TPU v7x, 32 devices: a whole 2x2x4 slice. The times are simulated.
32 devices in a mesh: grp: 2 (over y), freq: 4 (over z), ell: 2 (over x), pol: 2 (over core).
Axes of the slice: x: 2, y: 2, z: 4, core: 2. Of those that a mesh axis runs over, the one named last changes fastest.
Arguments:
- beam_matrix: bfloat16 [8, 2, 512, 8192], P(('grp', 'freq'), None, None, ('ell', 'pol')), parts along dimension 0, may hold values from -0.375 to 0.375
- sky_spectrum: float32 [8, 3, 8192], P(('grp', 'freq'), None, ('ell', 'pol')), parts along dimension 0, may hold values from 0.1 to 10
- taper_tiles: bfloat16 [3, 512, 512], P(None, ('ell', 'pol')), may hold values from 0.5 to 1.5
- noise_tiles: bfloat16 [8, 3, 512, 2, 512], P(('grp', 'freq'), None, ('ell', 'pol')), parts along dimension 0, may hold values from -4 to 4
Outputs:
- covariance: float32 [8, 3, 512, 2, 512], P(('grp', 'freq'), None, ('ell', 'pol')), parts along dimension 0
There are 2 independent parts, one for each index of `grp`. A program takes and returns all parts, laid end to end along the dimension named above; an argument that names none is the same for every part. Nothing has to cross between parts.
All inputs are finite; a program needn't handle non-finite values.
Results may differ from a plain program's by a relative error of at most 0.012.
Values may be sent and summed in bfloat16 or wider, within the bound.
A program may use at most 64 MiB of HBM per device.

v0:
```python
import jax
import jax.numpy as jnp
from jax import lax
from jax.sharding import PartitionSpec as P


def passed_along(block, axis, distance):
    devices = range(lax.axis_size(axis))
    route = [(i - distance, i) for i in devices if i - distance in devices]
    return lax.ppermute(block, axis, route)


def make_term(scaled, stacked_right, mode_count):

    def tile_term(first_row, row_count):
        real_rows = scaled[0]
        imag_rows = scaled[1]
        top_half = jnp.concatenate([real_rows, imag_rows], axis=-1)
        bottom_half = jnp.concatenate([imag_rows, -real_rows], axis=-1)
        left_rows = jnp.stack([top_half, bottom_half], axis=1).reshape(
            2 * row_count, top_half.shape[-1]
        )
        product = lax.dot_general(
            left_rows, stacked_right, (((1,), (1,)), ((), ())), preferred_element_type=jnp.float32
        )
        return product.reshape(row_count, 2, mode_count)

    return tile_term


def local(beam_matrix, sky_spectrum, taper_tiles, noise_tiles):
    per_device = beam_matrix.shape[0]
    mode_count = beam_matrix.shape[2]
    separations = sky_spectrum.shape[1]
    local_rows = taper_tiles.shape[1]
    needed = (per_device - 1 + separations) // per_device
    blocks = [beam_matrix]
    for offset in range(needed):
        blocks.append(passed_along(beam_matrix, "freq", -(offset + 1)))
    term_list = []
    for sep_index in range(separations):
        target = sep_index + 1
        partner = blocks[target // per_device][target % per_device]
        spec_row = sky_spectrum[0, sep_index]
        scaled = (spec_row[None, None, :] * beam_matrix[0].astype(jnp.float32)).astype(jnp.bfloat16)
        stacked_right = jnp.concatenate([partner[0], partner[1]], axis=-1)
        tile_term = make_term(scaled, stacked_right, mode_count)
        term_list.append(
            lax.psum_scatter(
                tile_term(jnp.int32(0), lax.axis_size(("ell", "pol")) * local_rows).astype(
                    jnp.bfloat16
                ),
                ("ell", "pol"),
                scatter_dimension=0,
                tiled=True,
            ).astype(jnp.float32)
        )
    summed = jnp.stack(term_list).reshape(per_device, separations, local_rows, 2, mode_count)
    result = taper_tiles.astype(jnp.float32)[None, :, :, None, :] * summed + noise_tiles.astype(
        jnp.float32
    )
    return result


def solution(mesh):
    placed = (
        P(("grp", "freq"), None, None, ("ell", "pol")),
        P(("grp", "freq"), None, ("ell", "pol")),
        P(None, ("ell", "pol"), None),
        P(("grp", "freq"), None, ("ell", "pol"), None, None),
    )
    return jax.shard_map(
        local,
        mesh=mesh,
        in_specs=placed,
        out_specs=P(("grp", "freq"), None, ("ell", "pol"), None, None),
        check_vma=False,
    )
```

profile of v0, /device:TPU:0, one launch (start us, length us, event | category | flops | bytes accessed | tf_op | source)
XLA Modules:
  0.0 442.0 jit_solution(7819483632951395245)
XLA Ops:
  6.5 0.0 reduce-scatter.4.cloned.1.call-start
  6.5 1.3 collective-permute-start
  7.8 1.3 collective-permute-start.1
  9.1 1.3 collective-permute-start.2
  10.4 0.7 fusion.36
  11.2 4.6 %fusion = (bf16[2,512,2048]{2,1,0:T(8,128)(2,1)S(1)}, bf16[2,512,2048]{2,1,0:T(8,128)(2,1)S(1)}, bf16[2,512,2048]{2,1,0:T(8,128)(2,1)S(1)}) fusion(bf16[1,2,512,2048]{3,2,1,0:T(8,128)(2,1)} %param.4, f32[2048]{0:T(1024)S(1)} %bitcast.71, f32[2048]{0:T(1024)S(1)} %bitcast.72, f32[2048]{0:T(1024)S(1)} %bitcast.73), kind=kLoop, calls=%fused_computation.3 | loop fusion | flops 14680064 | bytes 16801792 | tf_op jit(solution)/shard_map/convert_element_type | solution.py:45
  15.8 0.0 copy-start
  15.8 0.3 fusion.33
  16.1 0.6 slice_bitcast_fusion.11
  16.7 1.0 maximum_bitcast_fusion
  17.7 0.5 copy-done
  18.2 3.4 slice_bitcast_fusion.3
  21.6 80.7 %collective-permute-done = bf16[1,2,512,2048]{3,2,1,0:T(8,128)(2,1)S(1)} collective-permute-done((bf16[1,2,512,2048]{3,2,1,0:T(8,128)(2,1)}, bf16[1,2,512,2048]{3,2,1,0:T(8,128)(2,1)S(1)}, u32[]{:S(2)}, u32[]{:S(2)}) %collective-permute-start) | collective-permute-done | bytes 4194336 | tf_op jit(solution)/shard_map/ppermute | solution.py:10
  102.3 0.6 slice_bitcast_fusion.9
  102.8 5.5 %fusion.27 = bf16[512,2,512]{2,0,1:T(8,128)(2,1)} fusion(bf16[512,2048]{1,0:T(8,128)(2,1)S(1)} %get-tuple-element.11, bf16[512,2048]{1,0:T(8,128)(2,1)S(1)} %get-tuple-element.10, bf16[512,1,4096]{2,0,1:T(8,128)(2,1)S(1)} %get-tuple-element.21, bf16[512,1,4096]{2,0,1:T(8,128)(2,1)S(1)} %get-tuple-element.20), kind=kOutput, calls=%fused_computation.48 | convolution fusion | flops 4308074496 | bytes 13631488 | tf_op jit(solution)/shard_map/dot_general | solution.py:23
  108.3 0.0 reduce-scatter.4.cloned.1.call-update
  108.4 0.0 reduce-scatter.6.cloned.1.call-start
  108.4 0.0 copy-start.1
  108.4 3.3 maximum_bitcast_fusion.4
  111.7 0.7 copy-done.1
  112.5 0.1 fusion.35
  112.6 260.6 %collective-permute-done.1 = bf16[1,2,512,2048]{3,2,1,0:T(8,128)(2,1)} collective-permute-done((bf16[1,2,512,2048]{3,2,1,0:T(8,128)(2,1)}, bf16[1,2,512,2048]{3,2,1,0:T(8,128)(2,1)}, u32[]{:S(2)}, u32[]{:S(2)}) %collective-permute-start.1) | collective-permute-done | bytes 4194336 | tf_op jit(solution)/shard_map/ppermute | solution.py:10
  373.2 2.5 slice_bitcast_fusion.5
  375.7 5.5 %fusion.24 = bf16[512,2,512]{2,0,1:T(8,128)(2,1)} fusion(bf16[512,2048]{1,0:T(8,128)(2,1)S(1)} %get-tuple-element.15, bf16[512,2048]{1,0:T(8,128)(2,1)S(1)} %get-tuple-element.14, bf16[512,1,4096]{2,0,1:T(8,128)(2,1)S(1)} %get-tuple-element.23, bf16[512,1,4096]{2,0,1:T(8,128)(2,1)S(1)} %get-tuple-element.22), kind=kOutput, calls=%fused_computation.47 | convolution fusion | flops 4308074496 | bytes 13631488 | tf_op jit(solution)/shard_map/dot_general | solution.py:23
  381.2 0.0 reduce-scatter.6.cloned.1.call-update
  381.2 0.2 reduce-scatter.8.cloned.1.call-start
  381.5 3.2 maximum_bitcast_fusion.8
  384.7 0.0 collective-permute-done.2
  384.7 2.7 slice_bitcast_fusion.1
  387.3 0.0 copy-start.3
  387.3 0.0 copy-start.2
  387.3 5.5 %fusion.21 = bf16[512,2,512]{2,0,1:T(8,128)(2,1)} fusion(bf16[512,2048]{1,0:T(8,128)(2,1)S(1)} %get-tuple-element.19, bf16[512,2048]{1,0:T(8,128)(2,1)S(1)} %get-tuple-element.18, bf16[512,1,4096]{2,0,1:T(8,128)(2,1)S(1)} %get-tuple-element.25, bf16[512,1,4096]{2,0,1:T(8,128)(2,1)S(1)} %get-tuple-element.24), kind=kOutput, calls=%fused_computation.46 | convolution fusion | flops 4308074496 | bytes 13631488 | tf_op jit(solution)/shard_map/dot_general | solution.py:23
  392.8 0.0 reduce-scatter.8.cloned.1.call-update
  392.9 0.0 copy-done.3
  392.9 0.1 convert_element_type.35
  393.0 0.0 reduce-scatter.4.cloned.1.call-done
  393.0 11.4 %reduce-scatter.6.cloned.1.call-done = bf16[128,2,512]{2,0,1:T(8,128)(2,1)} async-done(((bf16[512,2,512]{2,0,1:T(8,128)(2,1)}), bf16[128,2,512]{2,0,1:T(8,128)(2,1)}) %reduce-scatter.6.cloned.1.call-update) | async-done | bytes 262160 | tf_op jit(solution)/shard_map/reduce_scatter | solution.py:49
  404.4 27.3 %reduce-scatter.8.cloned.1.call-done = bf16[128,2,512]{2,0,1:T(8,128)(2,1)} async-done(((bf16[512,2,512]{2,0,1:T(8,128)(2,1)}), bf16[128,2,512]{2,0,1:T(8,128)(2,1)}) %reduce-scatter.8.cloned.1.call-update) | async-done | bytes 262160 | tf_op jit(solution)/shard_map/reduce_scatter | solution.py:49
  431.7 0.0 copy-done.2
  431.7 1.4 convert_add_fusion
  433.1 2.4 copy.6
Async XLA Ops:
  6.5 386.5 %reduce-scatter.4.cloned.1.call-start = ((), (), s32[]{:S(2)}) async-start(), calls=%async_computation.3 | async-start | bytes 1310720 | tf_op jit(solution)/shard_map/reduce_scatter | solution.py:49
  6.5 95.7 %collective-permute-start = (bf16[1,2,512,2048]{3,2,1,0:T(8,128)(2,1)}, bf16[1,2,512,2048]{3,2,1,0:T(8,128)(2,1)S(1)}, u32[]{:S(2)}, u32[]{:S(2)}) collective-permute-start(bf16[1,2,512,2048]{3,2,1,0:T(8,128)(2,1)} %param.4), channel_id=1, source_target_pairs={{4,0},{8,4},{12,8},{5,1},{9,5},{13,9},{6,2},{10,6},{14,10},{7,3},{... | collective-permute-start | bytes 12582920 | tf_op jit(solution)/shard_map/ppermute | solution.py:10
  7.8 365.4 %collective-permute-start.1 = (bf16[1,2,512,2048]{3,2,1,0:T(8,128)(2,1)}, bf16[1,2,512,2048]{3,2,1,0:T(8,128)(2,1)}, u32[]{:S(2)}, u32[]{:S(2)}) collective-permute-start(bf16[1,2,512,2048]{3,2,1,0:T(8,128)(2,1)} %param.4), channel_id=1, source_target_pairs={{8,0},{12,4},{9,1},{13,5},{10,2},{14,6},{11,3},{15,7},{24,16},{28,... | collective-permute-start | bytes 12582920 | tf_op jit(solution)/shard_map/ppermute | solution.py:10
  9.1 375.5 %collective-permute-start.2 = (bf16[1,2,512,2048]{3,2,1,0:T(8,128)(2,1)}, bf16[1,2,512,2048]{3,2,1,0:T(8,128)(2,1)}, u32[]{:S(2)}, u32[]{:S(2)}) collective-permute-start(bf16[1,2,512,2048]{3,2,1,0:T(8,128)(2,1)} %param.4), channel_id=1, source_target_pairs={{12,0},{13,1},{14,2},{15,3},{28,16},{29,17},{30,18},{31,19}} | collective-permute-start | bytes 12582920 | tf_op jit(solution)/shard_map/ppermute | solution.py:10
  15.8 2.4 copy-start
  108.4 296.0 %reduce-scatter.6.cloned.1.call-start = ((), (), s32[]{:S(2)}) async-start(), calls=%async_computation.4 | async-start | bytes 1310720 | tf_op jit(solution)/shard_map/reduce_scatter | solution.py:49
  108.4 4.1 copy-start.1
  381.2 50.5 %reduce-scatter.8.cloned.1.call-start = ((), (), s32[]{:S(2)}) async-start(), calls=%async_computation.5 | async-start | bytes 1310720 | tf_op jit(solution)/shard_map/reduce_scatter | solution.py:49
  387.3 5.5 %copy-start.3 = (bf16[3,128,512]{2,1,0:T(8,128)(2,1)S(1)}, bf16[3,128,512]{2,1,0:T(8,128)(2,1)}, u32[]{:S(2)}) copy-start(bf16[3,128,512]{2,1,0:T(8,128)(2,1)} %param.6) | copy-start | bytes 1179652
  387.3 44.4 %copy-start.2 = (bf16[1,3,128,2,512]{4,3,2,1,0:T(2,128)(2,1)S(1)}, bf16[1,3,128,2,512]{4,3,2,1,0:T(2,128)(2,1)}, u32[]{:S(2)}) copy-start(bf16[1,3,128,2,512]{4,3,2,1,0:T(2,128)(2,1)} %param.7) | copy-start | bytes 2359300
Sparse Core Ops, SparseCore 0:
  108.5 205.0 reduce-scatter.3
  381.4 22.9 reduce-scatter.5
  406.9 24.7 reduce-scatter.7
where the time goes:
time: 442 us
  waiting for transfers between devices  380 us (86%)
  matrix products  16.5 us (4%)
  local copies, waits for them, and re-layouts  14.1 us (3%)
  other arithmetic  14 us (3%)
  between operations  13.3 us (3%)
    ppermute x3, waiting for transfers between devices, passed_along(): return lax.ppermute(block, axis, route)  341 us
    reduce_scatter x3, waiting for transfers between devices, local(): lax.psum_scatter(tile_term(jnp.int32(0), lax.axis_size(('ell', 'pol')) *...  38.7 us
    dot_general x3, matrix products, tile_term(): lax.dot_general(left_rows, stacked_right, (((1,), (1,)), ((), ())), prefe...  16.5 us
  transfers between devices with their start and end apart: 6, of which 4 were waited for; matrix products, arithmetic and copies ran while one was open for 9% of the time, Pallas kernels for 0%

commit v1 on v0

v1 whole, which is shorter than its diff:
```python
import functools

import jax
import jax.numpy as jnp
from jax import lax
from jax.experimental import pallas as pl
from jax.experimental.pallas import tpu as pltpu
from jax.sharding import PartitionSpec as P

CHUNKS = 4
LANES = 128


def passed_along(block, axis, distance):
    devices = range(lax.axis_size(axis))
    route = [(i - distance, i) for i in devices if i - distance in devices]
    return lax.ppermute(block, axis, route)


def general_sums(beam_matrix, sky_spectrum, local_rows):
    per_device = beam_matrix.shape[0]
    mode_count = beam_matrix.shape[2]
    separations = sky_spectrum.shape[1]
    needed = (per_device - 1 + separations) // per_device
    blocks = [beam_matrix]
    for offset in range(needed):
        blocks.append(passed_along(beam_matrix, "freq", -(offset + 1)))
    term_list = []
    for sep_index in range(separations):
        target = sep_index + 1
        partner = blocks[target // per_device][target % per_device]
        spec_row = sky_spectrum[0, sep_index]
        scaled = (spec_row[None, None, :] * beam_matrix[0].astype(jnp.float32)).astype(jnp.bfloat16)
        right = jnp.concatenate([partner[0], partner[1]], axis=-1)
        top = jnp.concatenate([scaled[0], scaled[1]], axis=-1)
        bottom = jnp.concatenate([scaled[1], -scaled[0]], axis=-1)
        left = jnp.stack([top, bottom], axis=1).reshape(2 * mode_count, top.shape[-1])
        product = lax.dot_general(
            left, right, (((1,), (1,)), ((), ())), preferred_element_type=jnp.float32
        ).reshape(mode_count, 2, mode_count)
        term_list.append(
            lax.psum_scatter(
                product.astype(jnp.bfloat16), ("ell", "pol"), scatter_dimension=0, tiled=True
            ).astype(jnp.float32)
        )
    return jnp.stack(term_list)


T12, T13, T02, T03, TEND = range(5)


def meet_kernel(
    cut, own, spec, out,
    outer, near, far, spec0, spec1, stage, inbox, back_out, back_in, final_out, final_in,
    spec_s, spec_r, near_s, near_r, o1_s, o1_r, o2_s, o2_r, fw_s, fw_r,
    rs_s, rs_r, bk_s, bk_r, fn_s, fn_r,
):
    f32, bf16 = jnp.float32, jnp.bfloat16
    _, groups, rows, width = own.shape
    modes = groups * rows
    chunks = CHUNKS
    step = rows // chunks
    freqs = lax.axis_size("freq")
    pols = lax.axis_size("pol")
    freq = lax.axis_index("freq")
    me = lax.axis_index("ell") * pols + lax.axis_index("pol")
    low, high, full = (0, cut), (cut, width), (0, width)
    every = slice(None)

    barrier = pltpu.get_barrier_semaphore()
    for d in range(1, freqs):
        pl.semaphore_signal(
            barrier, inc=1, device_id={"freq": lax.rem(freq + d, freqs)},
            device_id_type=pl.DeviceIdType.MESH,
        )
    for d in range(1, groups):
        other = lax.rem(me + d, groups)
        pl.semaphore_signal(
            barrier, inc=1, device_id={"ell": other // pols, "pol": lax.rem(other, pols)},
            device_id_type=pl.DeviceIdType.MESH,
        )
    pl.semaphore_wait(barrier, freqs - 1 + groups - 1)

    def span(c):
        return pl.ds(pl.multiple_of(c * step, step), step)

    def to_freq(src, dst, send, recv, target):
        return pltpu.make_async_remote_copy(
            src_ref=src, dst_ref=dst, send_sem=send, recv_sem=recv,
            device_id={"freq": target}, device_id_type=pl.DeviceIdType.MESH,
        )

    def lanes(part):
        return pl.ds(part[0], part[1] - part[0])

    def send_spec(n, src, dst, target):
        return to_freq(src, dst, spec_s.at[n], spec_r.at[n], target)

    def mid(part, target):
        where = (every, every, every, lanes(part))
        return to_freq(own.at[where], near.at[where], near_s.at[0], near_r.at[0], target)

    def row_chunk(c, part):
        return (every, every, span(c), lanes(part))

    def block_chunk(g, part):
        return (every, pl.ds(g, 1), every, lanes(part))

    def hop(src, dst, send, recv, c, where, target):
        return to_freq(src.at[where], dst.at[where], send.at[c], recv.at[c], target)

    def share(tile, piece, where):
        copies = []
        for d in range(1, groups):
            other = lax.rem(me + d, groups)
            copies.append(
                pltpu.make_async_remote_copy(
                    src_ref=stage.at[(tile, other) + where],
                    dst_ref=inbox.at[(tile, d - 1) + where],
                    send_sem=rs_s.at[tile, piece, d - 1],
                    recv_sem=rs_r.at[tile, piece, d - 1],
                    device_id={"ell": other // pols, "pol": lax.rem(other, pols)},
                    device_id_type=pl.DeviceIdType.MESH,
                )
            )
        return copies

    def start_share(tile, piece, where):
        for copy in share(tile, piece, where):
            copy.start()

    whole = (every, every, every)

    def rows_of(c):
        return (every, span(c), every)

    def cols_of(g):
        return (every, every, pl.ds(pl.multiple_of(g * rows, rows), rows))

    def dot(a, b):
        return lax.dot_general(a, b, (((1,), (1,)), ((), ())), preferred_element_type=f32)

    def scaled(block, part_index, where, weight):
        value = block[(part_index,) + where].reshape(-1, weight.shape[-1])
        return (weight * value.astype(f32)).astype(bf16)

    def cross(left, left_where, weight, right, right_where):
        a_re = scaled(left, 0, left_where, weight)
        a_im = scaled(left, 1, left_where, weight)
        b_re = right[(0,) + right_where].reshape(-1, weight.shape[-1])
        b_im = right[(1,) + right_where].reshape(-1, weight.shape[-1])
        real = dot(a_re, b_re) + dot(a_im, b_im)
        imag = dot(a_im, b_re) - dot(a_re, b_im)
        return real.astype(bf16), imag.astype(bf16)

    def by_rows(tile, c, left, weights, sep, right, part):
        weight = weights[pl.ds(sep, 1), lanes(part)]
        real, imag = cross(
            left, (every, span(c), lanes(part)), weight, right, (every, every, lanes(part))
        )
        stage[tile, :, 0, span(c), :] = real.reshape(groups, step, modes)
        stage[tile, :, 1, span(c), :] = imag.reshape(groups, step, modes)

    def by_columns(tile, g, left, weights, sep, right, part):
        weight = weights[pl.ds(sep, 1), lanes(part)]
        columns = pl.ds(pl.multiple_of(g * rows, rows), rows)

        def body(o, carry):
            real, imag = cross(
                left, (o, every, lanes(part)), weight, right, (g, every, lanes(part))
            )
            stage[tile, o, 0, :, columns] = real
            stage[tile, o, 1, :, columns] = imag
            return carry

        lax.fori_loop(0, groups, body, 0)

    def gathered(tile, piece, where):
        for copy in share(tile, piece, where):
            copy.wait_recv()
        total = stage[(tile, me) + where].astype(f32)
        for d in range(groups - 1):
            total = total + inbox[(tile, d) + where].astype(f32)
        return total

    def loop(lo, hi, body):
        def wrapped(i, carry):
            body(i)
            return carry

        lax.fori_loop(lo, hi, wrapped, 0)

    def settle(tile, pieces, where_of):
        def body(c):
            for copy in share(tile, c, where_of(c)):
                copy.wait_send()

        loop(0, pieces, body)

    def give_back(tile, c, where):
        return to_freq(
            back_out.at[(tile,) + where], back_in.at[(tile,) + where],
            bk_s.at[tile, c], bk_r.at[tile, c], 1,
        )

    def deliver(sep, c):
        where = rows_of(c)
        return to_freq(
            final_out.at[(sep,) + where], final_in.at[(sep,) + where],
            fn_s.at[sep, c], fn_r.at[sep, c], 0,
        )

    @pl.when(freq == 0)
    def _():
        send_spec(0, spec, spec0, 1).start()
        send_spec(1, spec, spec0, 2).start()
        loop(0, chunks, lambda c: hop(own, outer, o1_s, o1_r, c, row_chunk(c, high), 1).start())
        loop(0, chunks, lambda c: hop(own, outer, o2_s, o2_r, c, row_chunk(c, low), 1).start())
        send_spec(0, spec, spec0, 1).wait_send()
        send_spec(1, spec, spec0, 2).wait_send()
        loop(0, chunks, lambda c: hop(own, outer, o1_s, o1_r, c, row_chunk(c, high), 1).wait_send())
        loop(0, chunks, lambda c: hop(own, outer, o2_s, o2_r, c, row_chunk(c, low), 1).wait_send())
        for sep in range(3):
            loop(0, chunks, lambda c: deliver(sep, c).wait_recv())
            out[sep] = final_in[sep]

    @pl.when(freq == 3)
    def _():
        loop(0, groups, lambda g: hop(own, outer, o1_s, o1_r, g, block_chunk(g, low), 2).start())
        loop(0, groups, lambda g: hop(own, outer, o2_s, o2_r, g, block_chunk(g, high), 2).start())
        out[...] = jnp.zeros_like(out)
        loop(0, groups, lambda g: hop(own, outer, o1_s, o1_r, g, block_chunk(g, low), 2).wait_send())
        loop(0, groups, lambda g: hop(own, outer, o2_s, o2_r, g, block_chunk(g, high), 2).wait_send())

    @pl.when(freq == 1)
    def _():
        send_spec(2, spec, spec1, 2).start()
        mid(high, 2).start()

        def relay(c):
            hop(own, outer, o1_s, o1_r, c, row_chunk(c, high), 1).wait_recv()
            hop(outer, far, fw_s, fw_r, c, row_chunk(c, high), 2).start()

        loop(0, chunks - 1, relay)
        mid(low, 1).wait_recv()
        loop(0, chunks, lambda c: by_rows(T12, c, own, spec, 0, near, low))
        start_share(T12, 0, whole)
        loop(chunks - 1, chunks, relay)
        send_spec(0, spec, spec0, 1).wait_recv()

        def finish_end(c):
            final_out[(0,) + rows_of(c)] = gathered(TEND, c, rows_of(c)).astype(bf16)
            deliver(0, c).start()

        def take(c):
            hop(own, outer, o2_s, o2_r, c, row_chunk(c, low), 1).wait_recv()
            by_rows(TEND, c, outer, spec0, 0, own, full)
            start_share(TEND, c, rows_of(c))
            by_rows(T02, c, outer, spec0, 1, near, low)
            start_share(T02, c, rows_of(c))

            @pl.when(c == chunks - 2)
            def _():
                loop(0, groups, lambda g: hop(
                    outer, far, fw_s, fw_r, g, block_chunk(g, low), 1).wait_recv())
                loop(0, chunks, lambda r: by_rows(T13, r, own, spec, 1, far, low))
                start_share(T13, 0, whole)

            def last(r):
                by_rows(T03, r, outer, spec0, 2, far, low)
                start_share(T03, r, rows_of(r))

            first = jnp.where(c == chunks - 2, 0, c)
            stop = jnp.where(c >= chunks - 2, c + 1, 0)
            loop(first, stop, last)
            loop(jnp.maximum(c - 1, 0), c, finish_end)

        loop(0, chunks, take)
        loop(chunks - 1, chunks, finish_end)

        def settled(tile, where):
            return gathered(tile, 0, where) + back_in[(tile,) + where].astype(f32)

        def cross_end(tile, sep):
            def body(c):
                where = rows_of(c)
                total = gathered(tile, c, where)
                give_back(tile, c, where).wait_recv()
                total = total + back_in[(tile,) + where].astype(f32)
                final_out[(sep,) + where] = total.astype(bf16)
                deliver(sep, c).start()

            return body

        give_back(T12, 0, whole).wait_recv()
        out[0] = settled(T12, whole).astype(bf16)
        loop(0, chunks - 1, cross_end(T02, 1))
        give_back(T13, 0, whole).wait_recv()
        out[1] = settled(T13, whole).astype(bf16)
        out[2] = jnp.zeros(out.shape[1:], bf16)
        loop(0, chunks - 1, cross_end(T03, 2))
        loop(chunks - 1, chunks, cross_end(T02, 1))
        loop(chunks - 1, chunks, cross_end(T03, 2))

        send_spec(2, spec, spec1, 2).wait_send()
        mid(high, 2).wait_send()
        loop(0, chunks, lambda c: hop(outer, far, fw_s, fw_r, c, row_chunk(c, high), 2).wait_send())
        for tile, pieces, where_of in (
            (T12, 1, lambda c: whole), (T13, 1, lambda c: whole),
            (T02, chunks, rows_of), (T03, chunks, rows_of), (TEND, chunks, rows_of),
        ):
            settle(tile, pieces, where_of)
        for sep in range(3):
            loop(0, chunks, lambda c: deliver(sep, c).wait_send())

    @pl.when(freq == 2)
    def _():
        mid(low, 1).start()

        def relay(g):
            hop(own, outer, o1_s, o1_r, g, block_chunk(g, low), 2).wait_recv()
            hop(outer, far, fw_s, fw_r, g, block_chunk(g, low), 1).start()

        loop(0, groups, relay)
        send_spec(1, spec, spec0, 2).wait_recv()
        send_spec(2, spec, spec1, 2).wait_recv()
        mid(high, 2).wait_recv()
        loop(0, chunks, lambda c: by_rows(T12, c, near, spec1, 0, own, high))
        start_share(T12, 0, whole)

        def return_rows(tile):
            def body(c):
                where = rows_of(c)
                back_out[(tile,) + where] = gathered(tile, c, where).astype(bf16)
                give_back(tile, c, where).start()

            return body

        def row_product(tile, sep, right):
            def body(c):
                by_rows(tile, c, far, spec0, sep, right, high)
                start_share(tile, c, rows_of(c))

            return body

        def take_columns(g):
            hop(own, outer, o2_s, o2_r, g, block_chunk(g, high), 2).wait_recv()
            by_columns(T13, g, near, spec1, 1, outer, high)
            start_share(T13, g, cols_of(g))
            by_columns(TEND, g, own, spec, 0, outer, full)
            start_share(TEND, g, cols_of(g))

        def return_first():
            back_out[T12] = gathered(T12, 0, whole).astype(bf16)
            give_back(T12, 0, whole).start()

        steps = max(groups, chunks)

        def take(c):
            if groups == steps:
                take_columns(c)
            else:
                loop(c, jnp.minimum(c + 1, groups), take_columns)

            @pl.when(c == 0)
            def _():
                return_first()

            @pl.when(c == steps - 1)
            def _():
                loop(0, chunks - 1, row_product(T03, 2, outer))
                loop(0, groups, return_columns)
                give_back(T13, 0, whole).start()
                loop(0, chunks - 1, return_rows(T03))

            hop(outer, far, fw_s, fw_r, c, row_chunk(c, high), 2).wait_recv()
            row_product(T02, 1, own)(c)

            @pl.when(c == steps - 1)
            def _():
                row_product(T03, 2, outer)(c)

            loop(jnp.maximum(c - 1, 0), c, return_rows(T02))

        def return_columns(g):
            where = cols_of(g)
            back_out[(T13,) + where] = gathered(T13, g, where).astype(bf16)

        loop(0, steps, take)
        loop(chunks - 1, chunks, return_rows(T02))
        loop(chunks - 1, chunks, return_rows(T03))

        def end_columns(g):
            where = cols_of(g)
            out[(0,) + where] = gathered(TEND, g, where).astype(bf16)

        loop(0, groups, end_columns)
        out[1] = jnp.zeros(out.shape[1:], bf16)
        out[2] = jnp.zeros(out.shape[1:], bf16)

        mid(low, 1).wait_send()
        loop(0, groups, lambda g: hop(outer, far, fw_s, fw_r, g, block_chunk(g, low), 1).wait_send())
        for tile, pieces, where_of in (
            (T12, 1, lambda c: whole), (T13, groups, cols_of),
            (T02, chunks, rows_of), (T03, chunks, rows_of), (TEND, groups, cols_of),
        ):
            settle(tile, pieces, where_of)
        give_back(T12, 0, whole).wait_send()
        give_back(T13, 0, whole).wait_send()
        loop(0, chunks, lambda c: give_back(T02, c, rows_of(c)).wait_send())
        loop(0, chunks, lambda c: give_back(T03, c, rows_of(c)).wait_send())


def meet_sums(beam_matrix, sky_spectrum, local_rows):
    _, parts, modes, width = beam_matrix.shape
    separations = sky_spectrum.shape[1]
    groups = modes // local_rows
    tiles = 4 * 2 * local_rows * modes
    block = parts * modes * width
    cut = int(width * (0.5 - tiles / (4 * block))) // LANES * LANES
    pieces = max(CHUNKS, groups)
    bf16 = jnp.bfloat16
    shape = (parts, groups, local_rows, width)
    tile = (2, local_rows, modes)
    dma = pltpu.SemaphoreType.DMA
    pair = lambda *dims: [dma(dims), dma(dims)]
    return pl.pallas_call(
        functools.partial(meet_kernel, cut),
        out_shape=jax.ShapeDtypeStruct((separations,) + tile, bf16),
        in_specs=[pl.BlockSpec(memory_space=pltpu.VMEM)] * 2,
        out_specs=pl.BlockSpec(memory_space=pltpu.VMEM),
        scratch_shapes=[
            pltpu.VMEM(shape, bf16),
            pltpu.VMEM(shape, bf16),
            pltpu.VMEM(shape, bf16),
            pltpu.VMEM(sky_spectrum.shape[1:], jnp.float32),
            pltpu.VMEM(sky_spectrum.shape[1:], jnp.float32),
            pltpu.VMEM((5, groups) + tile, bf16),
            pltpu.VMEM((5, groups - 1) + tile, bf16),
            pltpu.VMEM((4,) + tile, bf16),
            pltpu.VMEM((4,) + tile, bf16),
            pltpu.VMEM((3,) + tile, bf16),
            pltpu.VMEM((3,) + tile, bf16),
            *pair(3), *pair(1), *pair(pieces), *pair(pieces), *pair(pieces),
            *pair(5, pieces, groups - 1), *pair(4, pieces), *pair(3, pieces),
        ],
        compiler_params=pltpu.CompilerParams(
            collective_id=0, has_side_effects=True, vmem_limit_bytes=60 * 2**20
        ),
    )(beam_matrix[0].reshape(shape), sky_spectrum[0])


def local(beam_matrix, sky_spectrum, taper_tiles, noise_tiles):
    per_device, _, modes, width = beam_matrix.shape
    separations = sky_spectrum.shape[1]
    local_rows = taper_tiles.shape[1]
    in_line = (
        per_device == 1
        and separations == 3
        and lax.axis_size("freq") == separations + 1
        and modes // local_rows == CHUNKS
        and local_rows % LANES == 0
        and width % (8 * LANES) == 0
    )
    if in_line:
        summed = meet_sums(beam_matrix, sky_spectrum, local_rows)
        summed = jnp.swapaxes(summed, 1, 2).astype(jnp.float32)
    else:
        summed = general_sums(beam_matrix, sky_spectrum, local_rows)
    summed = summed.reshape(per_device, separations, local_rows, 2, modes)
    taper = taper_tiles.astype(jnp.float32)[None, :, :, None, :]
    return taper * summed + noise_tiles.astype(jnp.float32)


def solution(mesh):
    placed = (
        P(("grp", "freq"), None, None, ("ell", "pol")),
        P(("grp", "freq"), None, ("ell", "pol")),
        P(None, ("ell", "pol"), None),
        P(("grp", "freq"), None, ("ell", "pol"), None, None),
    )
    return jax.shard_map(
        local,
        mesh=mesh,
        in_specs=placed,
        out_specs=P(("grp", "freq"), None, ("ell", "pol"), None, None),
        check_vma=False,
    )
```

time: 442 us -> 148 us (0.33)
  waiting for transfers between devices: 380 us -> 0 us
  Pallas kernels: 0 us -> 142 us
  matrix products: 16.5 us -> 0 us
  other arithmetic: 14 us -> 0.38 us
  between operations: 13.3 us -> 0.05 us
  local copies, waits for them, and re-layouts: 14.1 us -> 4.76 us
    ppermute x3 -> x0, waiting for transfers between devices: 341 us -> none  [passed_along(): return lax.ppermute(block, axis, route)]
    pallas_call x0 -> x1, Pallas kernels: none -> 142 us  [meet_sums(): pl.pallas_call(functools.partial(meet_kernel, cut), out_shape=jax.ShapeDt...]
    reduce_scatter x3 -> x0, waiting for transfers between devices: 38.7 us -> none  [local(): lax.psum_scatter(tile_term(jnp.int32(0), lax.axis_size(('ell', 'pol')) *...]
    dot_general x3 -> x0, matrix products: 16.5 us -> none  [tile_term(): lax.dot_general(left_rows, stacked_right, (((1,), (1,)), ((), ())), prefe...]
    squeeze x5 -> x0, local copies, waits for them, and re-layouts: 9.69 us -> none  [the longest x3 5.76 us: local(): stacked_right = jnp.concatenate([partner[0], partner[1]], axis=-1)]
    another operation x3 -> x0, other arithmetic: 7.51 us -> none  [tile_term(): jnp.stack([top_half, bottom_half], axis=1)]
    convert_element_type x2 -> x1, other arithmetic: 4.72 us -> 0.08 us  [local(): taper = taper_tiles.astype(jnp.float32)[None, :, :, None, :]]
  transfers between devices with their start and end apart: 6 -> 0, of which waited for: 4 -> 0; matrix products, arithmetic and copies ran while one was open for 9% -> 0% of each run, Pallas kernels for 0% -> 0%
where the time goes in v1:
time: 148 us
  Pallas kernels  142 us (96%)
  local copies, waits for them, and re-layouts  4.76 us (3%)
    pallas_call x1, Pallas kernels, meet_sums(): pl.pallas_call(functools.partial(meet_kernel, cut), out_shape=jax.ShapeDt...  142 us

profile of v1, /device:TPU:0, one launch (start us, length us, event | category | flops | bytes accessed | tf_op | source)
XLA Modules:
  0.0 147.5 jit_solution(7256318313544448015)
XLA Ops:
  0.0 1.4 copy.10
  1.4 0.0 copy-start.2
  1.4 0.0 copy-start.1
  1.4 142.3 %shard_map.46 = bf16[3,2,128,512]{3,2,1,0:T(8,128)(2,1)} custom-call(bf16[2,4,128,2048]{3,2,1,0:T(8,128)(2,1)} %bitcast.8, f32[3,2048]{1,0:T(4,128)} %bitcast.9), custom_call_target="tpu_custom_call" | custom-call | tf_op jit(solution)/shard_map/pallas_call | solution.py:427
  143.7 0.0 copy-done.2
  143.7 0.0 copy-start
  143.7 0.1 convert_element_type.10
  143.8 0.0 copy-done.1
  143.8 1.0 copy-done
  144.8 0.3 bitcast_add_fusion
  145.1 2.4 %copy.6 = f32[1,3,128,2,512]{4,3,2,1,0:T(2,128)} copy(f32[1,3,128,2,512]{4,2,3,1,0:T(8,128)S(1)} %bitcast_add_fusion) | data formatting | bytes 3145728 | tf_op jit(solution)/shard_map/add | solution.py:472
Async XLA Ops:
  1.4 142.3 %copy-start.2 = (bf16[3,128,512]{2,1,0:T(8,128)(2,1)S(1)}, bf16[3,128,512]{2,1,0:T(8,128)(2,1)}, u32[]{:S(2)}) copy-start(bf16[3,128,512]{2,1,0:T(8,128)(2,1)} %param.6) | copy-start | bytes 1179652
  1.4 142.4 %copy-start.1 = (bf16[1,3,128,2,512]{4,3,2,1,0:T(2,128)(2,1)S(1)}, bf16[1,3,128,2,512]{4,3,2,1,0:T(2,128)(2,1)}, u32[]{:S(2)}) copy-start(bf16[1,3,128,2,512]{4,3,2,1,0:T(2,128)(2,1)} %param.7) | copy-start | bytes 2359300
  143.7 1.1 copy-start

commit v2 on v1

--- a/solution.py
+++ b/solution.py
@@ -200,7 +200,7 @@
     def give_back(tile, c, where):
         return to_freq(
             back_out.at[(tile,) + where], back_in.at[(tile,) + where],
-            bk_s.at[tile, c], bk_r.at[tile, c], 1,
+            bk_s.at[tile, c], bk_r.at[tile, c], 0 if tile in (T02, T03) else 1,
         )
 
     def deliver(sep, c):
@@ -220,9 +220,18 @@
         send_spec(1, spec, spec0, 2).wait_send()
         loop(0, chunks, lambda c: hop(own, outer, o1_s, o1_r, c, row_chunk(c, high), 1).wait_send())
         loop(0, chunks, lambda c: hop(own, outer, o2_s, o2_r, c, row_chunk(c, low), 1).wait_send())
-        for sep in range(3):
-            loop(0, chunks, lambda c: deliver(sep, c).wait_recv())
-            out[sep] = final_in[sep]
+
+        def land(c):
+            for sep, tile in ((1, T02), (2, T03)):
+                where = rows_of(c)
+                deliver(sep, c).wait_recv()
+                give_back(tile, c, where).wait_recv()
+                total = final_in[(sep,) + where].astype(f32) + back_in[(tile,) + where].astype(f32)
+                out[(sep,) + where] = total.astype(bf16)
+
+        loop(0, chunks, lambda c: deliver(0, c).wait_recv())
+        out[0] = final_in[0]
+        loop(0, chunks, land)
 
     @pl.when(freq == 3)
     def _():
@@ -252,6 +261,25 @@
             final_out[(0,) + rows_of(c)] = gathered(TEND, c, rows_of(c)).astype(bf16)
             deliver(0, c).start()
 
+        def cross_end(tile, sep):
+            def body(c):
+                where = rows_of(c)
+                final_out[(sep,) + where] = gathered(tile, c, where).astype(bf16)
+                deliver(sep, c).start()
+
+            return body
+
+        def block_in(g):
+            hop(outer, far, fw_s, fw_r, g, block_chunk(g, low), 1).wait_recv()
+
+        def columns_end(g):
+            by_columns(T13, g, own, spec, 1, far, low)
+            start_share(T13, g, cols_of(g))
+
+        def near_end(g):
+            block_in(g)
+            columns_end(g)
+
         def take(c):
             hop(own, outer, o2_s, o2_r, c, row_chunk(c, low), 1).wait_recv()
             by_rows(TEND, c, outer, spec0, 0, own, full)
@@ -259,54 +287,44 @@
             by_rows(T02, c, outer, spec0, 1, near, low)
             start_share(T02, c, rows_of(c))
 
-            @pl.when(c == chunks - 2)
-            def _():
-                loop(0, groups, lambda g: hop(
-                    outer, far, fw_s, fw_r, g, block_chunk(g, low), 1).wait_recv())
-                loop(0, chunks, lambda r: by_rows(T13, r, own, spec, 1, far, low))
-                start_share(T13, 0, whole)
-
             def last(r):
                 by_rows(T03, r, outer, spec0, 2, far, low)
                 start_share(T03, r, rows_of(r))
 
             first = jnp.where(c == chunks - 2, 0, c)
             stop = jnp.where(c >= chunks - 2, c + 1, 0)
+            loop(c, jnp.where(c < chunks - 2, c + 1, c), near_end)
+            loop(chunks - 2, jnp.where(c == chunks - 2, chunks, 0), block_in)
             loop(first, stop, last)
-            loop(jnp.maximum(c - 1, 0), c, finish_end)
+            before = jnp.maximum(c - 1, 0)
+            loop(before, c, finish_end)
+            loop(before, c, cross_end(T02, 1))
+            loop(0, jnp.where(c == chunks - 1, c, 0), cross_end(T03, 2))
 
         loop(0, chunks, take)
+        loop(chunks - 2, chunks, columns_end)
         loop(chunks - 1, chunks, finish_end)
 
-        def settled(tile, where):
-            return gathered(tile, 0, where) + back_in[(tile,) + where].astype(f32)
-
-        def cross_end(tile, sep):
-            def body(c):
-                where = rows_of(c)
-                total = gathered(tile, c, where)
-                give_back(tile, c, where).wait_recv()
-                total = total + back_in[(tile,) + where].astype(f32)
-                final_out[(sep,) + where] = total.astype(bf16)
-                deliver(sep, c).start()
-
-            return body
-
-        give_back(T12, 0, whole).wait_recv()
-        out[0] = settled(T12, whole).astype(bf16)
-        loop(0, chunks - 1, cross_end(T02, 1))
-        give_back(T13, 0, whole).wait_recv()
-        out[1] = settled(T13, whole).astype(bf16)
-        out[2] = jnp.zeros(out.shape[1:], bf16)
-        loop(0, chunks - 1, cross_end(T03, 2))
         loop(chunks - 1, chunks, cross_end(T02, 1))
         loop(chunks - 1, chunks, cross_end(T03, 2))
+        out[2] = jnp.zeros(out.shape[1:], bf16)
+        give_back(T12, 0, whole).wait_recv()
+        total = gathered(T12, 0, whole) + back_in[T12].astype(f32)
+        out[0] = total.astype(bf16)
+        give_back(T13, 0, whole).wait_recv()
+
+        def own_columns(g):
+            where = cols_of(g)
+            total = gathered(T13, g, where) + back_in[(T13,) + where].astype(f32)
+            out[(1,) + where] = total.astype(bf16)
+
+        loop(0, groups, own_columns)
 
         send_spec(2, spec, spec1, 2).wait_send()
         mid(high, 2).wait_send()
         loop(0, chunks, lambda c: hop(outer, far, fw_s, fw_r, c, row_chunk(c, high), 2).wait_send())
         for tile, pieces, where_of in (
-            (T12, 1, lambda c: whole), (T13, 1, lambda c: whole),
+            (T12, 1, lambda c: whole), (T13, groups, cols_of),
             (T02, chunks, rows_of), (T03, chunks, rows_of), (TEND, chunks, rows_of),
         ):
             settle(tile, pieces, where_of)
@@ -343,50 +361,46 @@
 
             return body
 
+        def end_product(g):
+            by_columns(TEND, g, own, spec, 0, outer, full)
+            start_share(TEND, g, cols_of(g))
+
         def take_columns(g):
             hop(own, outer, o2_s, o2_r, g, block_chunk(g, high), 2).wait_recv()
             by_columns(T13, g, near, spec1, 1, outer, high)
             start_share(T13, g, cols_of(g))
-            by_columns(TEND, g, own, spec, 0, outer, full)
-            start_share(TEND, g, cols_of(g))
-
-        def return_first():
-            back_out[T12] = gathered(T12, 0, whole).astype(bf16)
-            give_back(T12, 0, whole).start()
-
-        steps = max(groups, chunks)
+            loop(g, jnp.minimum(g + 1, groups - 1), end_product)
+
+        per = chunks // groups
+        late = chunks - per
 
         def take(c):
-            if groups == steps:
-                take_columns(c)
-            else:
-                loop(c, jnp.minimum(c + 1, groups), take_columns)
+            due = jnp.where(lax.rem(c, per) == 0, 1, 0)
+            loop(c // per, c // per + due, take_columns)
 
             @pl.when(c == 0)
             def _():
-                return_first()
-
-            @pl.when(c == steps - 1)
+                back_out[T12] = gathered(T12, 0, whole).astype(bf16)
+                give_back(T12, 0, whole).start()
+
+            @pl.when(c == late)
             def _():
-                loop(0, chunks - 1, row_product(T03, 2, outer))
+                loop(0, late, row_product(T03, 2, outer))
                 loop(0, groups, return_columns)
                 give_back(T13, 0, whole).start()
-                loop(0, chunks - 1, return_rows(T03))
 
             hop(outer, far, fw_s, fw_r, c, row_chunk(c, high), 2).wait_recv()
             row_product(T02, 1, own)(c)
-
-            @pl.when(c == steps - 1)
-            def _():
-                row_product(T03, 2, outer)(c)
-
+            loop(c, jnp.where(c >= late, c + 1, c), row_product(T03, 2, outer))
             loop(jnp.maximum(c - 1, 0), c, return_rows(T02))
+            loop(jnp.where(c == late, 0, jnp.maximum(c - 1, 0)), jnp.where(c >= late, c, 0), return_rows(T03))
 
         def return_columns(g):
             where = cols_of(g)
             back_out[(T13,) + where] = gathered(T13, g, where).astype(bf16)
 
-        loop(0, steps, take)
+        loop(0, chunks, take)
+        loop(groups - 1, groups, end_product)
         loop(chunks - 1, chunks, return_rows(T02))
         loop(chunks - 1, chunks, return_rows(T03))
 

time: 148 us -> 137 us (0.926)
  Pallas kernels: 142 us -> 131 us
    pallas_call x1, Pallas kernels: 142 us -> 131 us  [meet_sums(): pl.pallas_call(functools.partial(meet_kernel, cut), out_shape=jax.ShapeDt...]
where the time goes in v2:
time: 137 us
  Pallas kernels  131 us (96%)
  local copies, waits for them, and re-layouts  4.76 us (3%)
    pallas_call x1, Pallas kernels, meet_sums(): pl.pallas_call(functools.partial(meet_kernel, cut), out_shape=jax.ShapeDt...  131 us

profile of v2, /device:TPU:0, one launch (start us, length us, event | category | flops | bytes accessed | tf_op | source)
XLA Modules:
  0.0 136.5 jit_solution(1136774264788361176)
XLA Ops:
  0.0 1.4 copy.10
  1.4 0.0 copy-start.2
  1.4 0.0 copy-start.1
  1.4 131.3 %shard_map.46 = bf16[3,2,128,512]{3,2,1,0:T(8,128)(2,1)} custom-call(bf16[2,4,128,2048]{3,2,1,0:T(8,128)(2,1)} %bitcast.8, f32[3,2048]{1,0:T(4,128)} %bitcast.9), custom_call_target="tpu_custom_call" | custom-call | tf_op jit(solution)/shard_map/pallas_call | solution.py:441
  132.7 0.0 copy-done.2
  132.7 0.0 copy-start
  132.7 0.1 convert_element_type.10
  132.8 0.0 copy-done.1
  132.8 1.0 copy-done
  133.9 0.3 bitcast_add_fusion
  134.2 2.4 %copy.6 = f32[1,3,128,2,512]{4,3,2,1,0:T(2,128)} copy(f32[1,3,128,2,512]{4,2,3,1,0:T(8,128)S(1)} %bitcast_add_fusion) | data formatting | bytes 3145728 | tf_op jit(solution)/shard_map/add | solution.py:486
Async XLA Ops:
  1.4 131.3 %copy-start.2 = (bf16[3,128,512]{2,1,0:T(8,128)(2,1)S(1)}, bf16[3,128,512]{2,1,0:T(8,128)(2,1)}, u32[]{:S(2)}) copy-start(bf16[3,128,512]{2,1,0:T(8,128)(2,1)} %param.6) | copy-start | bytes 1179652
  1.4 131.5 %copy-start.1 = (bf16[1,3,128,2,512]{4,3,2,1,0:T(2,128)(2,1)S(1)}, bf16[1,3,128,2,512]{4,3,2,1,0:T(2,128)(2,1)}, u32[]{:S(2)}) copy-start(bf16[1,3,128,2,512]{4,3,2,1,0:T(2,128)(2,1)} %param.7) | copy-start | bytes 2359300
  132.7 1.1 copy-start
